TPU v7x, 32 devices: a whole 2x2x4 slice. The times are simulated.
32 devices in a mesh: row: 4 (over x, core), tile: 8 (over z, y).
Axes of the slice: x: 2, y: 2, z: 4, core: 2. Of those that a mesh axis runs over, the one named last changes fastest.
Arguments:
- currents: bfloat16 [2, 4, 2, 128, 8192], P(None, None, None, ('row', 'tile')), may hold values from -6 to 6
- row_angles: int32 [2048], replicated, may hold values from 0 to 32767
- column_angles: int32 [2048], replicated, may hold values from 0 to 32767
- target: float32 [2, 2048, 2048], P(None, 'tile', 'row'), may hold values from 2 to 14
- weight: float32 [2, 2048, 2048], P(None, 'tile', 'row'), may hold values from 0.01 to 0.1
- tile_owner: int32 [8192, 1], P(('row', 'tile')), may hold values from 0 to 31; in each aligned block of 256 rows (0 to 255, 256 to 511, ...) at most 16 rows name the same one
- face_slot: int32 [8192], P(('row', 'tile')), may hold values from 0 to 255
Outputs:
- intensity: float32 [2, 2048, 2048], P(None, 'tile', 'row')
- faces: float32 [2, 4, 2, 8192, 128], P(None, None, None, ('row', 'tile'))
Inputs may be any that keep to these rules, and one draw needn't show every extreme that they name: `tile_owner`: among the 256 segments of one device no owner is named more than 16 times, a bound that some block reaches.
All inputs are finite; a program needn't handle non-finite values.
Results may differ from a plain program's by a relative error of at most 0.0085.
Values may be sent and summed in bfloat16 or wider, within the bound.
No kernel may reach another device: no remote copies, remote signals or barrier semaphores. Data moves between devices by JAX's collectives and lax.ppermute only.
A program may use at most 128 MiB of HBM per device.

v0:
```python
import math
import jax
import jax.numpy as jnp
from jax import lax
from jax.sharding import PartitionSpec as P

SEG = 128


def phase_pair(position, angles, modulus, scale):
    turns = position[:, None] * angles[None, :] % modulus
    angle = turns.astype(jnp.float32) * (2.0 * math.pi / modulus)
    return (jnp.cos(angle) * scale, jnp.sin(angle) * scale)


def spread_back(half):
    return jnp.stack([half[:, 0], half[:, 1], -half[:, 1], half[:, 0]], axis=1)


def polarize(fields):
    return jnp.stack([fields[:, 0] + fields[:, 3], fields[:, 1] - fields[:, 2]], axis=1)


def body(currents, row_angles, column_angles, target, weight, tile_owner, face_slot):
    row_count = lax.axis_size("row")
    tile_count = lax.axis_size("tile")
    devices = row_count * tile_count
    freq_count, comp_count, part_count, rows_dev, columns = currents.shape
    far_rows = row_angles.shape[0]
    far_cols = column_angles.shape[0]
    share_cols = far_cols // tile_count
    modulus = 4 * columns
    column_scale = 1.0 / math.sqrt(columns)
    row_scale = 1.0 / math.sqrt(rows_dev * devices)
    block_width = min(512, far_cols)
    block_count = far_cols // block_width
    channel_count = freq_count * comp_count
    column_index = jnp.arange(columns, dtype=jnp.int32)
    channels = currents.reshape(channel_count * part_count, rows_dev, columns)

    def column_block(offset):
        angles = lax.dynamic_slice_in_dim(column_angles, offset, block_width)
        cos_part, sin_part = phase_pair(column_index, angles, modulus, column_scale)
        return (cos_part.astype(jnp.bfloat16), sin_part.astype(jnp.bfloat16))

    def forward_step(state, offset):
        cos_part, sin_part = column_block(offset)
        table = jnp.stack([cos_part, sin_part], axis=1)
        products = jnp.einsum("qxy,ysv->qsvx", channels, table, preferred_element_type=jnp.float32)
        products = products.reshape(channel_count, 2, 2, block_width, rows_dev)
        real_part = products[:, 0, 0] + products[:, 1, 1]
        imag_part = products[:, 1, 0] - products[:, 0, 1]
        return (state, jnp.stack([real_part, imag_part], axis=1).astype(jnp.bfloat16))

    block_starts = jnp.arange(block_count, dtype=jnp.int32) * block_width
    _, column_pieces = lax.scan(forward_step, jnp.int32(0), block_starts)
    ordered_cols = jnp.moveaxis(column_pieces, 0, 2)
    plane_cols = ordered_cols.reshape(channel_count * part_count, tile_count, share_cols * rows_dev)
    received = lax.all_to_all(plane_cols, "tile", split_axis=1, concat_axis=1, tiled=True)
    received = received.reshape(channel_count, 2, tile_count, share_cols, rows_dev)
    here_row = lax.axis_index("row")
    group_pos = here_row * (tile_count * rows_dev) + jnp.arange(
        tile_count * rows_dev, dtype=jnp.int32
    )
    row_cos, row_sin = phase_pair(group_pos, row_angles, modulus, row_scale)
    row_cos = row_cos.astype(jnp.bfloat16).reshape(tile_count, rows_dev, far_rows)
    row_sin = row_sin.astype(jnp.bfloat16).reshape(tile_count, rows_dev, far_rows)
    table_real = jnp.stack([row_cos, row_sin])
    table_imag = jnp.stack([-row_sin, row_cos])
    field_re = jnp.einsum(
        "qrtvx,rtxu->qvu", received, table_real, preferred_element_type=jnp.float32
    )
    field_im = jnp.einsum(
        "qrtvx,rtxu->qvu", received, table_imag, preferred_element_type=jnp.float32
    )
    field_re = field_re.reshape(freq_count, comp_count, share_cols, far_rows)
    field_im = field_im.reshape(freq_count, comp_count, share_cols, far_rows)
    fields = jnp.stack([field_re, field_im], axis=2)
    own_fields = polarize(lax.psum_scatter(fields, "row", scatter_dimension=4, tiled=True))
    intensity = jnp.sum(own_fields * own_fields, axis=(1, 2))
    factor = 4.0 * weight * (intensity - target)
    far_grad = (factor[:, None, None] * own_fields).astype(jnp.bfloat16)
    portion = lax.all_gather(far_grad, "row", axis=4, tiled=True)
    extent = portion.shape[4]
    angles = row_angles
    piece_cos, piece_sin = phase_pair(group_pos, angles, modulus, row_scale)
    piece_cos = piece_cos.astype(jnp.bfloat16).reshape(tile_count, rows_dev, extent)
    piece_sin = piece_sin.astype(jnp.bfloat16).reshape(tile_count, rows_dev, extent)
    back_real = jnp.stack([piece_cos, -piece_sin])
    back_imag = jnp.stack([piece_sin, piece_cos])
    next_re = jnp.einsum(
        "fprvu,rtxu->fptvx", portion, back_real, preferred_element_type=jnp.float32
    )
    next_im = jnp.einsum(
        "fprvu,rtxu->fptvx", portion, back_imag, preferred_element_type=jnp.float32
    )
    back_re = next_re
    back_im = next_im
    plane_grad = jnp.stack([spread_back(back_re), spread_back(back_im)], axis=2).astype(
        jnp.bfloat16
    )
    plane_grad = plane_grad.reshape(channel_count * part_count, tile_count, share_cols * rows_dev)
    returned = lax.all_to_all(plane_grad, "tile", split_axis=1, concat_axis=1, tiled=True)
    returned = returned.reshape(channel_count, 2, far_cols, rows_dev)

    def adjoint_step(totals, offset):
        cos_part, sin_part = column_block(offset)
        grad_block = lax.dynamic_slice_in_dim(returned, offset, block_width, axis=2)
        with_cos = jnp.einsum(
            "qrvx,yv->qrxy", grad_block, cos_part, preferred_element_type=jnp.float32
        )
        with_sin = jnp.einsum(
            "qrvx,yv->qrxy", grad_block, sin_part, preferred_element_type=jnp.float32
        )
        next_re = totals[0] + with_cos[:, 0] - with_sin[:, 1]
        next_im = totals[1] + with_sin[:, 0] + with_cos[:, 1]
        return ((next_re, next_im), None)

    plane_zero = jnp.zeros((channel_count, rows_dev, columns), jnp.float32)
    (adjoint_re, adjoint_im), _ = lax.scan(adjoint_step, (plane_zero, plane_zero), block_starts)
    adjoint = jnp.stack([adjoint_re, adjoint_im], axis=1).astype(jnp.bfloat16)
    segments = adjoint.reshape(channel_count * part_count, rows_dev * columns // SEG, SEG)
    seg_count = segments.shape[1]
    capacity = max(2, 2 * seg_count // devices)
    owner_index = tile_owner[:, 0]
    matches = (owner_index[:, None] == jnp.arange(devices, dtype=jnp.int32)[None, :]).astype(
        jnp.int32
    )
    earlier = jnp.cumsum(matches, axis=0) - matches
    ranked = jnp.sum(earlier * matches, axis=1)
    position = owner_index * capacity + ranked
    outgoing = jnp.zeros((channel_count * part_count, devices * capacity, SEG), jnp.bfloat16)
    outgoing = outgoing.at[:, position].set(segments)
    labels = jnp.full((devices * capacity,), seg_count, jnp.int32).at[position].set(face_slot)
    arrived, slot_marks = (
        lax.all_to_all(
            outgoing.reshape(channel_count * part_count, devices, capacity, SEG),
            ("row", "tile"),
            split_axis=1,
            concat_axis=1,
            tiled=True,
        ),
        lax.all_to_all(
            labels.reshape(1, devices, capacity),
            ("row", "tile"),
            split_axis=1,
            concat_axis=1,
            tiled=True,
        ),
    )
    arrived = arrived.reshape(channel_count * part_count, devices * capacity, SEG).astype(
        jnp.float32
    )
    slot_marks = slot_marks.reshape(devices * capacity)
    faces = jnp.zeros((channel_count * part_count, seg_count, SEG), jnp.float32)
    faces = faces.at[:, slot_marks].add(arrived, mode="drop")
    return (intensity, faces.reshape(freq_count, comp_count, part_count, seg_count, SEG))


def solution(mesh):
    in_specs = (
        P(None, None, None, ("row", "tile"), None),
        P(),
        P(),
        P(None, "tile", "row"),
        P(None, "tile", "row"),
        P(("row", "tile"), None),
        P(("row", "tile")),
    )
    out_specs = (P(None, "tile", "row"), P(None, None, None, ("row", "tile"), None))
    return jax.shard_map(body, mesh=mesh, in_specs=in_specs, out_specs=out_specs, check_vma=False)
```

profile of v0, /device:TPU:0, one launch (start us, length us, event | category | flops | bytes accessed | tf_op | source)
XLA Modules:
  0.0 1409.9 jit_solution(18253644668635062543)
XLA Ops:
  9.0 300.6 %while.28 = (s32[]{:T(128)}, bf16[4,8,2,512,4]{3,1,4,2,0:T(8,128)(2,1)S(1)}, s32[4]{0:T(128)S(1)}, s32[2048]{0:T(1024)}, bf16[16,4,8192]{2,0,1:T(8,128)(2,1)S(1)}, /*index=5*/s32[]{:T(128)}, s32[]{:T(128)}, s32[]{:T(128)}) while((s32[]{:T(128)}, bf16[4,8,2,512,4]{3,1,4,2,0:T(8,128)(2,1)S(1)}, s32[4]{0:T(128)S(1)}, s32[2048]{0:T(1024)}, ...), condition=%wide.region_1.2_spmd.clone, body=%wide.region_0.1_spmd.clone.sunk | while | flops 1182990336 | bytes 36378764 | solution.py:56
  12.3 67.9 %multiply_convert_fusion.8 = (bf16[8192,1,512]{2,0,1:T(8,128)(2,1)S(1)}, bf16[8192,1,512]{2,0,1:T(8,128)(2,1)S(1)}) fusion(s32[512]{0:T(512)S(1)} %dynamic_slice.53), kind=kLoop, calls=%fused_computation.16.clone.1 | loop fusion | flops 75497472 | bytes 16779264 | tf_op jit(solution)/shard_map/while/body/eval_jaxpr/convert_element_type | solution.py:44
  87.5 67.9 %multiply_convert_fusion.8 = (bf16[8192,1,512]{2,0,1:T(8,128)(2,1)S(1)}, bf16[8192,1,512]{2,0,1:T(8,128)(2,1)S(1)}) fusion(s32[512]{0:T(512)S(1)} %dynamic_slice.53), kind=kLoop, calls=%fused_computation.16.clone.1 | loop fusion | flops 75497472 | bytes 16779264 | tf_op jit(solution)/shard_map/while/body/eval_jaxpr/convert_element_type | solution.py:44
  162.6 67.9 %multiply_convert_fusion.8 = (bf16[8192,1,512]{2,0,1:T(8,128)(2,1)S(1)}, bf16[8192,1,512]{2,0,1:T(8,128)(2,1)S(1)}) fusion(s32[512]{0:T(512)S(1)} %dynamic_slice.53), kind=kLoop, calls=%fused_computation.16.clone.1 | loop fusion | flops 75497472 | bytes 16779264 | tf_op jit(solution)/shard_map/while/body/eval_jaxpr/convert_element_type | solution.py:44
  237.7 67.9 %multiply_convert_fusion.8 = (bf16[8192,1,512]{2,0,1:T(8,128)(2,1)S(1)}, bf16[8192,1,512]{2,0,1:T(8,128)(2,1)S(1)}) fusion(s32[512]{0:T(512)S(1)} %dynamic_slice.53), kind=kLoop, calls=%fused_computation.16.clone.1 | loop fusion | flops 75497472 | bytes 16779264 | tf_op jit(solution)/shard_map/while/body/eval_jaxpr/convert_element_type | solution.py:44
  309.6 6.0 copy.43
  315.6 17.0 %reshape.427 = bf16[16,8,1024]{2,1,0:T(8,128)(2,1)S(1)} reshape(bf16[8,2,4,512,4]{4,3,2,1,0:T(8,128)(2,1)} %copy.43) | data formatting | bytes 524288 | tf_op jit(solution)/shard_map/reshape | solution.py:58
  333.5 7.3 all-to-all-start
  343.3 6.3 all-to-all-done
  352.8 5.2 copy.46
  362.8 11.7 pad_maximum_fusion
  375.0 233.4 %reduce-scatter.2.cloned.1.call-done = f32[2,4,2,256,512]{4,3,1,0,2:T(8,128)} async-done(((f32[2,4,2,256,2048]{4,3,1,0,2:T(8,128)}), f32[2,4,2,256,512]{4,3,1,0,2:T(8,128)}) %reduce-scatter.2.cloned.1.call-update) | async-done | bytes 8388624 | tf_op jit(solution)/shard_map/reduce_scatter | solution.py:79
  617.0 58.4 %all-gather.2.cloned.1.call-done = bf16[2,2,2,256,2048]{4,3,1,0,2:T(8,128)(2,1)} async-done(((bf16[2,2,2,256,512]{4,3,1,0,2:T(8,128)(2,1)}), bf16[2,2,2,256,2048]{4,3,1,0,2:T(8,128)(2,1)}) %all-gather.2.cloned.1.call-update) | async-done | bytes 8388624 | tf_op jit(solution)/shard_map/all_gather | solution.py:83
  675.4 6.0 fusion.87
  684.2 4.5 copy.53
  693.2 5.5 all-to-all-start.2
  701.9 6.1 all-to-all-done.2
  711.3 19.0 %reshape.433 = bf16[8,2,2048,4]{3,2,1,0:T(8,128)(2,1)} reshape(bf16[16,8,1024]{2,1,0:T(8,128)(2,1)S(1)} %copy.55) | data formatting | bytes 524288 | tf_op jit(solution)/shard_map/reshape | solution.py:104
  730.3 7.1 copy.56
  737.4 532.7 %while.29 = (s32[]{:T(128)}, f32[8,4,8192]{2,0,1:T(8,128)S(1)}, f32[8,4,8192]{2,0,1:T(8,128)}, s32[4]{0:T(128)S(1)}, bf16[8,2,2048,4]{2,0,3,1:T(8,128)(2,1)S(1)}...) while((s32[]{:T(128)}, f32[8,4,8192]{2,0,1:T(8,128)S(1)}, f32[8,4,8192]{2,0,1:T(8,128)}, ...), condition=%wide.region_9.10_spmd.clone, body=%wide.region_8.9_spmd.clone.sunk | while | flops 1209532416 | bytes 12722337 | solution.py:120
  740.9 62.6 %fusion.123 = f32[8,2,4,8192]{3,0,2,1:T(8,128)S(1)} fusion(s32[512]{0:T(512)S(1)} %dynamic_slice.57, bf16[8,2,2048,4]{2,0,3,1:T(8,128)(2,1)S(1)} %get-tuple-element.405, s32[]{:T(128)S(6)} %select_n.142), kind=kOutput, calls=%fused_computation.44.clone.3 | convolution fusion | flops 603979776 | bytes 2164740 | tf_op jit(solution)/shard_map/while/body/eval_jaxpr/qrvx,yv->qrxy/dot_general | solution.py:112
  803.5 63.4 %fusion.122 = f32[8,2,4,8192]{3,0,2,1:T(8,128)} fusion(s32[512]{0:T(512)S(1)} %dynamic_slice.57, bf16[8,2,2048,4]{2,0,3,1:T(8,128)(2,1)S(1)} %get-tuple-element.405, s32[]{:T(128)S(6)} %select_n.142), kind=kOutput, calls=%fused_computation.42.clone.3 | convolution fusion | flops 603979776 | bytes 2164740 | tf_op jit(solution)/shard_map/while/body/eval_jaxpr/qrvx,yv->qrxy/dot_general | solution.py:109
  873.8 62.6 %fusion.123 = f32[8,2,4,8192]{3,0,2,1:T(8,128)S(1)} fusion(s32[512]{0:T(512)S(1)} %dynamic_slice.57, bf16[8,2,2048,4]{2,0,3,1:T(8,128)(2,1)S(1)} %get-tuple-element.405, s32[]{:T(128)S(6)} %select_n.142), kind=kOutput, calls=%fused_computation.44.clone.3 | convolution fusion | flops 603979776 | bytes 2164740 | tf_op jit(solution)/shard_map/while/body/eval_jaxpr/qrvx,yv->qrxy/dot_general | solution.py:112
  936.3 63.4 %fusion.122 = f32[8,2,4,8192]{3,0,2,1:T(8,128)} fusion(s32[512]{0:T(512)S(1)} %dynamic_slice.57, bf16[8,2,2048,4]{2,0,3,1:T(8,128)(2,1)S(1)} %get-tuple-element.405, s32[]{:T(128)S(6)} %select_n.142), kind=kOutput, calls=%fused_computation.42.clone.3 | convolution fusion | flops 603979776 | bytes 2164740 | tf_op jit(solution)/shard_map/while/body/eval_jaxpr/qrvx,yv->qrxy/dot_general | solution.py:109
  1006.9 62.6 %fusion.123 = f32[8,2,4,8192]{3,0,2,1:T(8,128)S(1)} fusion(s32[512]{0:T(512)S(1)} %dynamic_slice.57, bf16[8,2,2048,4]{2,0,3,1:T(8,128)(2,1)S(1)} %get-tuple-element.405, s32[]{:T(128)S(6)} %select_n.142), kind=kOutput, calls=%fused_computation.44.clone.3 | convolution fusion | flops 603979776 | bytes 2164740 | tf_op jit(solution)/shard_map/while/body/eval_jaxpr/qrvx,yv->qrxy/dot_general | solution.py:112
  1069.5 63.4 %fusion.122 = f32[8,2,4,8192]{3,0,2,1:T(8,128)} fusion(s32[512]{0:T(512)S(1)} %dynamic_slice.57, bf16[8,2,2048,4]{2,0,3,1:T(8,128)(2,1)S(1)} %get-tuple-element.405, s32[]{:T(128)S(6)} %select_n.142), kind=kOutput, calls=%fused_computation.42.clone.3 | convolution fusion | flops 603979776 | bytes 2164740 | tf_op jit(solution)/shard_map/while/body/eval_jaxpr/qrvx,yv->qrxy/dot_general | solution.py:109
  1140.1 62.6 %fusion.123 = f32[8,2,4,8192]{3,0,2,1:T(8,128)S(1)} fusion(s32[512]{0:T(512)S(1)} %dynamic_slice.57, bf16[8,2,2048,4]{2,0,3,1:T(8,128)(2,1)S(1)} %get-tuple-element.405, s32[]{:T(128)S(6)} %select_n.142), kind=kOutput, calls=%fused_computation.44.clone.3 | convolution fusion | flops 603979776 | bytes 2164740 | tf_op jit(solution)/shard_map/while/body/eval_jaxpr/qrvx,yv->qrxy/dot_general | solution.py:112
  1202.6 63.4 %fusion.122 = f32[8,2,4,8192]{3,0,2,1:T(8,128)} fusion(s32[512]{0:T(512)S(1)} %dynamic_slice.57, bf16[8,2,2048,4]{2,0,3,1:T(8,128)(2,1)S(1)} %get-tuple-element.405, s32[]{:T(128)S(6)} %select_n.142), kind=kOutput, calls=%fused_computation.42.clone.3 | convolution fusion | flops 603979776 | bytes 2164740 | tf_op jit(solution)/shard_map/while/body/eval_jaxpr/qrvx,yv->qrxy/dot_general | solution.py:109
  1275.8 25.5 %scatter_fusion = bf16[16,512,128]{2,0,1:T(8,128)(2,1)} fusion(bf16[16,512,128]{2,0,1:T(8,128)(2,1)} %broadcast_in_dim.14, s32[256]{0:T(256)S(1)} %bitcast.193, bf16[256,16,128]{2,1,0:T(8,128)(2,1)S(1)} %copy.58), kind=kCustom, calls=%fused_computation.1 | custom fusion | bytes 3146752 | tf_op jit(solution)/shard_map/scatter | solution.py:133
  1301.3 5.8 all-to-all-start.3
  1309.2 48.0 %all-to-all-done.3 = bf16[16,32,16,128]{3,0,2,1:T(8,128)(2,1)S(1)} async-done(((bf16[16,32,16,128]{3,0,2,1:T(8,128)(2,1)}), bf16[16,32,16,128]{3,0,2,1:T(8,128)(2,1)S(1)}, u32[]{:S(2)}, u32[]{:S(2)}) %all-to-all-start.3) | async-done | bytes 2097184 | tf_op jit(solution)/shard_map/all_to_all | solution.py:136
  1359.8 41.0 %scatter_fusion.1 = f32[16,256,128]{2,0,1:T(8,128)S(1)} fusion(f32[16,256,128]{2,0,1:T(8,128)S(1)} %broadcast_in_dim.13, s32[512]{0:T(512)S(1)} %bitcast.191, f32[512,16,128]{2,1,0:T(8,128)} %convert_bitcast_fusion), kind=kCustom, calls=%fused_computation.2 | custom fusion | flops 1048576 | bytes 12584960 | tf_op jit(solution)/shard_map/scatter-add | solution.py:156
  (114 shorter events, 89.1 us)
Async XLA Ops:
  309.6 31.5 %copy-start.3 = (s32[2048]{0:T(1024)S(1)}, s32[2048]{0:T(1024)}, u32[]{:S(2)}) copy-start(s32[2048]{0:T(1024)} %param.12) | copy-start | bytes 24580
  333.5 16.2 %all-to-all-start = ((bf16[16,8,1024]{2,0,1:T(8,128)(2,1)}), bf16[16,8,1024]{2,0,1:T(8,128)(2,1)S(1)}, u32[]{:S(2)}, u32[]{:S(2)}) async-start(bf16[16,8,1024]{2,0,1:T(8,128)(2,1)} %copy.44), calls=%async_computation | async-start | bytes 524288 | tf_op jit(solution)/shard_map/all_to_all | solution.py:59
  340.8 267.7 %reduce-scatter.2.cloned.1.call-start = ((), (), s32[]{:S(2)}) async-start(), calls=%async_computation.5 | async-start | bytes 41943040 | tf_op jit(solution)/shard_map/reduce_scatter | solution.py:79
  374.5 240.0 %copy-start.1 = (f32[2,256,512]{2,1,0:T(8,128)S(1)}, f32[2,256,512]{2,1,0:T(8,128)}, u32[]{:S(2)}) copy-start(f32[2,256,512]{2,1,0:T(8,128)} %param.14) | copy-start | bytes 3145732
  374.5 240.0 %copy-start.2 = (f32[2,256,512]{2,1,0:T(8,128)S(1)}, f32[2,256,512]{2,1,0:T(8,128)}, u32[]{:S(2)}) copy-start(f32[2,256,512]{2,1,0:T(8,128)} %param.15) | copy-start | bytes 3145732
  374.5 300.9 %all-gather.2.cloned.1.call-start = ((), (), s32[]{:S(2)}) async-start(), calls=%async_computation.6 | async-start | bytes 10485760 | tf_op jit(solution)/shard_map/all_gather | solution.py:83
  613.5 1.0 copy-start
  675.4 6.1 slice-start
  675.4 6.1 slice-start.1
  684.0 14.6 %copy-start.4 = (s32[256,1]{0,1:T(1,128)S(1)}, s32[256,1]{0,1:T(1,128)}, u32[]{:S(2)}) copy-start(s32[256,1]{0,1:T(1,128)} %param.16) | copy-start | bytes 3076
  693.2 14.9 %all-to-all-start.2 = ((bf16[16,8,1024]{2,0,1:T(8,128)(2,1)}), bf16[16,8,1024]{2,0,1:T(8,128)(2,1)S(1)}, u32[]{:S(2)}, u32[]{:S(2)}) async-start(bf16[16,8,1024]{2,0,1:T(8,128)(2,1)} %copy.54), calls=%async_computation.3 | async-start | bytes 524288 | tf_op jit(solution)/shard_map/all_to_all | solution.py:103
  699.6 8.4 copy-start.5
  708.0 593.3 %all-to-all-start.1 = ((s32[1,32,16]{2,0,1:T(1,128)}), s32[1,32,16]{2,0,1:T(1,128)}, u32[]{:S(2)}, u32[]{:S(2)}) async-start(s32[1,32,16]{2,0,1:T(1,128)} %bitcast.20), calls=%async_computation.2 | async-start | bytes 32768 | tf_op jit(solution)/shard_map/all_to_all | solution.py:143
  1270.1 5.7 copy-start.6
  1301.3 55.9 %all-to-all-start.3 = ((bf16[16,32,16,128]{3,0,2,1:T(8,128)(2,1)}), bf16[16,32,16,128]{3,0,2,1:T(8,128)(2,1)S(1)}, u32[]{:S(2)}, u32[]{:S(2)}) async-start(bf16[16,32,16,128]{3,0,2,1:T(8,128)(2,1)} %bitcast.40), calls=%async_computation.4 | async-start | bytes 4194304 | tf_op jit(solution)/shard_map/all_to_all | solution.py:136
Sparse Core Ops, SparseCore 0:
  374.6 233.7 reduce-scatter.1
  617.1 58.2 all-gather.1
where the time goes:
time: 1420 us; the launch traced here: 1410 us
  matrix products  531 us (37%)
  other arithmetic  356 us (25%)
  waiting for transfers between devices  352 us (25%)
  local copies, waits for them, and re-layouts  118 us (8%)
  starting transfers between devices  22.4 us (2%)
  loops' own time  16.2 us (1%)
  between operations  14.8 us (1%)
    convert_element_type x4, other arithmetic, column_block(): return (cos_part.astype(jnp.bfloat16), sin_part.astype(jnp.bfloat16))  272 us
    dot_general x4, matrix products, adjoint_step(): jnp.einsum('qrvx,yv->qrxy', grad_block, cos_part, preferred_element_type=...  254 us
    dot_general x4, matrix products, adjoint_step(): jnp.einsum('qrvx,yv->qrxy', grad_block, sin_part, preferred_element_type=...  250 us
    reduce_scatter x1, waiting for transfers between devices, body(): lax.psum_scatter(fields, 'row', scatter_dimension=4, tiled=True)  233 us
    all_gather x1, waiting for transfers between devices, body(): portion = lax.all_gather(far_grad, 'row', axis=4, tiled=True)  58.4 us
    all_to_all x1, waiting for transfers between devices, body(): lax.all_to_all(outgoing.reshape(channel_count * part_count, devices, capa...  48 us
    scatter-add x1, other arithmetic, body(): faces = faces.at[:, slot_marks].add(arrived, mode='drop')  41 us
  transfers between devices with their start and end apart: 6, of which 5 were waited for; matrix products, arithmetic and copies ran while one was open for 42% of the time, Pallas kernels for 0%

commit v1 on v0

--- a/solution.py
+++ b/solution.py
@@ -133,12 +133,20 @@
     outgoing = outgoing.at[:, position].set(segments)
     labels = jnp.full((devices * capacity,), seg_count, jnp.int32).at[position].set(face_slot)
     arrived, slot_marks = (
-        lax.all_to_all(
-            outgoing.reshape(channel_count * part_count, devices, capacity, SEG),
-            ("row", "tile"),
-            split_axis=1,
-            concat_axis=1,
-            tiled=True,
+        jnp.concatenate(
+            lax.all_to_all(
+                jnp.stack(
+                    jnp.split(
+                        outgoing.reshape(channel_count * part_count, devices, capacity, SEG),
+                        lax.axis_size(("row", "tile")),
+                        axis=1,
+                    )
+                ),
+                ("row", "tile"),
+                0,
+                0,
+            ),
+            axis=1,
         ),
         lax.all_to_all(
             labels.reshape(1, devices, capacity),

time: 1420 us -> 1410 us (level)
    unnamed x20 -> x51, local copies, waits for them, and re-layouts: 10.1 us -> 29.7 us
    scatter x1, local copies, waits for them, and re-layouts: 25.5 us -> 7.06 us  [body(): outgoing = outgoing.at[:, position].set(segments)]
where the time goes in v1:
time: 1410 us
  matrix products  531 us (38%)
  other arithmetic  356 us (25%)
  waiting for transfers between devices  353 us (25%)
  local copies, waits for them, and re-layouts  112 us (8%)
  starting transfers between devices  22.6 us (2%)
  loops' own time  16.2 us (1%)
  between operations  14.8 us (1%)
    convert_element_type x4, other arithmetic, column_block(): return (cos_part.astype(jnp.bfloat16), sin_part.astype(jnp.bfloat16))  272 us
    dot_general x4, matrix products, adjoint_step(): jnp.einsum('qrvx,yv->qrxy', grad_block, cos_part, preferred_element_type=...  254 us
    dot_general x4, matrix products, adjoint_step(): jnp.einsum('qrvx,yv->qrxy', grad_block, sin_part, preferred_element_type=...  250 us
    reduce_scatter x1, waiting for transfers between devices, body(): lax.psum_scatter(fields, 'row', scatter_dimension=4, tiled=True)  233 us
    all_gather x1, waiting for transfers between devices, body(): portion = lax.all_gather(far_grad, 'row', axis=4, tiled=True)  58.4 us
    all_to_all x1, waiting for transfers between devices, body(): lax.all_to_all(jnp.stack(jnp.split(outgoing.reshape(channel_count * part_...  48.2 us
    scatter-add x1, other arithmetic, body(): faces = faces.at[:, slot_marks].add(arrived, mode='drop')  41 us
    unnamed x51, local copies, waits for them, and re-layouts  29.7 us
  transfers between devices with their start and end apart: 6, of which 5 were waited for; matrix products, arithmetic and copies ran while one was open for 42% of the time, Pallas kernels for 0%

profile of v1, /device:TPU:0, one launch (start us, length us, event | category | flops | bytes accessed | tf_op | source)
XLA Modules:
  0.0 1405.1 jit_solution(13566668627208986877)
XLA Ops:
  9.0 297.9 %while.28 = (s32[]{:T(128)}, bf16[4,8,2,512,4]{3,1,4,2,0:T(8,128)(2,1)S(1)}, s32[4]{0:T(128)S(1)}, s32[2048]{0:T(1024)S(1)}, bf16[16,4,8192]{2,0,1:T(8,128)(2,1)S(1)}, /*index=5*/s32[]{:T(128)}, s32[]{:T(128)}, s32[]{:T(128)}) while((s32[]{:T(128)}, bf16[4,8,2,512,4]{3,1,4,2,0:T(8,128)(2,1)S(1)}, s32[4]{0:T(128)S(1)}, ...), condition=%wide.region_1.2_spmd.clone, body=%wide.region_0.1_spmd.clone.sunk | while | flops 1182990336 | bytes 36378764 | solution.py:56
  11.6 68.0 %multiply_convert_fusion.8 = (bf16[8192,1,512]{2,0,1:T(8,128)(2,1)S(1)}, bf16[8192,1,512]{2,0,1:T(8,128)(2,1)S(1)}) fusion(s32[512]{0:T(512)S(1)} %dynamic_slice.53), kind=kLoop, calls=%fused_computation.16.clone.1 | loop fusion | flops 75497472 | bytes 16779264 | tf_op jit(solution)/shard_map/while/body/eval_jaxpr/convert_element_type | solution.py:44
  86.1 68.0 %multiply_convert_fusion.8 = (bf16[8192,1,512]{2,0,1:T(8,128)(2,1)S(1)}, bf16[8192,1,512]{2,0,1:T(8,128)(2,1)S(1)}) fusion(s32[512]{0:T(512)S(1)} %dynamic_slice.53), kind=kLoop, calls=%fused_computation.16.clone.1 | loop fusion | flops 75497472 | bytes 16779264 | tf_op jit(solution)/shard_map/while/body/eval_jaxpr/convert_element_type | solution.py:44
  160.6 68.0 %multiply_convert_fusion.8 = (bf16[8192,1,512]{2,0,1:T(8,128)(2,1)S(1)}, bf16[8192,1,512]{2,0,1:T(8,128)(2,1)S(1)}) fusion(s32[512]{0:T(512)S(1)} %dynamic_slice.53), kind=kLoop, calls=%fused_computation.16.clone.1 | loop fusion | flops 75497472 | bytes 16779264 | tf_op jit(solution)/shard_map/while/body/eval_jaxpr/convert_element_type | solution.py:44
  235.1 68.0 %multiply_convert_fusion.8 = (bf16[8192,1,512]{2,0,1:T(8,128)(2,1)S(1)}, bf16[8192,1,512]{2,0,1:T(8,128)(2,1)S(1)}) fusion(s32[512]{0:T(512)S(1)} %dynamic_slice.53), kind=kLoop, calls=%fused_computation.16.clone.1 | loop fusion | flops 75497472 | bytes 16779264 | tf_op jit(solution)/shard_map/while/body/eval_jaxpr/convert_element_type | solution.py:44
  306.9 6.0 copy.43
  312.9 17.0 %reshape.427 = bf16[16,8,1024]{2,1,0:T(8,128)(2,1)S(1)} reshape(bf16[8,2,4,512,4]{4,3,2,1,0:T(8,128)(2,1)} %copy.43) | data formatting | bytes 524288 | tf_op jit(solution)/shard_map/reshape | solution.py:58
  330.8 7.3 all-to-all-start
  340.7 6.3 all-to-all-done
  350.1 5.2 copy.46
  360.1 11.6 pad_maximum_fusion
  372.3 233.4 %reduce-scatter.2.cloned.1.call-done = f32[2,4,2,256,512]{4,3,1,0,2:T(8,128)} async-done(((f32[2,4,2,256,2048]{4,3,1,0,2:T(8,128)}), f32[2,4,2,256,512]{4,3,1,0,2:T(8,128)}) %reduce-scatter.2.cloned.1.call-update) | async-done | bytes 8388624 | tf_op jit(solution)/shard_map/reduce_scatter | solution.py:79
  614.3 58.4 %all-gather.2.cloned.1.call-done = bf16[2,2,2,256,2048]{4,3,1,0,2:T(8,128)(2,1)} async-done(((bf16[2,2,2,256,512]{4,3,1,0,2:T(8,128)(2,1)}), bf16[2,2,2,256,2048]{4,3,1,0,2:T(8,128)(2,1)}) %all-gather.2.cloned.1.call-update) | async-done | bytes 8388624 | tf_op jit(solution)/shard_map/all_gather | solution.py:83
  672.8 6.0 fusion.87
  681.5 4.5 copy.53
  690.4 5.5 all-to-all-start.2
  699.2 6.1 all-to-all-done.2
  708.7 19.0 %reshape.433 = bf16[8,2,2048,4]{3,2,1,0:T(8,128)(2,1)} reshape(bf16[16,8,1024]{2,1,0:T(8,128)(2,1)S(1)} %copy.55) | data formatting | bytes 524288 | tf_op jit(solution)/shard_map/reshape | solution.py:104
  727.7 7.1 copy.56
  734.8 529.9 %while.29 = (s32[]{:T(128)}, f32[8,4,8192]{2,0,1:T(8,128)S(1)}, f32[8,4,8192]{2,0,1:T(8,128)}, s32[4]{0:T(128)S(1)}, bf16[8,2,2048,4]{2,0,3,1:T(8,128)(2,1)S(1)}...) while((s32[]{:T(128)}, f32[8,4,8192]{2,0,1:T(8,128)S(1)}, f32[8,4,8192]{2,0,1:T(8,128)}, ...), condition=%wide.region_9.10_spmd.clone, body=%wide.region_8.9_spmd.clone.sunk | while | flops 1209532416 | bytes 12722337 | solution.py:120
  737.6 62.6 %fusion.123 = f32[8,2,4,8192]{3,0,2,1:T(8,128)S(1)} fusion(s32[512]{0:T(512)S(1)} %dynamic_slice.57, bf16[8,2,2048,4]{2,0,3,1:T(8,128)(2,1)S(1)} %get-tuple-element.405, s32[]{:T(128)S(6)} %select_n.142), kind=kOutput, calls=%fused_computation.44.clone.3 | convolution fusion | flops 603979776 | bytes 2164740 | tf_op jit(solution)/shard_map/while/body/eval_jaxpr/qrvx,yv->qrxy/dot_general | solution.py:112
  800.2 63.4 %fusion.122 = f32[8,2,4,8192]{3,0,2,1:T(8,128)} fusion(s32[512]{0:T(512)S(1)} %dynamic_slice.57, bf16[8,2,2048,4]{2,0,3,1:T(8,128)(2,1)S(1)} %get-tuple-element.405, s32[]{:T(128)S(6)} %select_n.142), kind=kOutput, calls=%fused_computation.42.clone.3 | convolution fusion | flops 603979776 | bytes 2164740 | tf_op jit(solution)/shard_map/while/body/eval_jaxpr/qrvx,yv->qrxy/dot_general | solution.py:109
  869.8 62.6 %fusion.123 = f32[8,2,4,8192]{3,0,2,1:T(8,128)S(1)} fusion(s32[512]{0:T(512)S(1)} %dynamic_slice.57, bf16[8,2,2048,4]{2,0,3,1:T(8,128)(2,1)S(1)} %get-tuple-element.405, s32[]{:T(128)S(6)} %select_n.142), kind=kOutput, calls=%fused_computation.44.clone.3 | convolution fusion | flops 603979776 | bytes 2164740 | tf_op jit(solution)/shard_map/while/body/eval_jaxpr/qrvx,yv->qrxy/dot_general | solution.py:112
  932.3 63.4 %fusion.122 = f32[8,2,4,8192]{3,0,2,1:T(8,128)} fusion(s32[512]{0:T(512)S(1)} %dynamic_slice.57, bf16[8,2,2048,4]{2,0,3,1:T(8,128)(2,1)S(1)} %get-tuple-element.405, s32[]{:T(128)S(6)} %select_n.142), kind=kOutput, calls=%fused_computation.42.clone.3 | convolution fusion | flops 603979776 | bytes 2164740 | tf_op jit(solution)/shard_map/while/body/eval_jaxpr/qrvx,yv->qrxy/dot_general | solution.py:109
  1002.2 62.6 %fusion.123 = f32[8,2,4,8192]{3,0,2,1:T(8,128)S(1)} fusion(s32[512]{0:T(512)S(1)} %dynamic_slice.57, bf16[8,2,2048,4]{2,0,3,1:T(8,128)(2,1)S(1)} %get-tuple-element.405, s32[]{:T(128)S(6)} %select_n.142), kind=kOutput, calls=%fused_computation.44.clone.3 | convolution fusion | flops 603979776 | bytes 2164740 | tf_op jit(solution)/shard_map/while/body/eval_jaxpr/qrvx,yv->qrxy/dot_general | solution.py:112
  1064.8 63.4 %fusion.122 = f32[8,2,4,8192]{3,0,2,1:T(8,128)} fusion(s32[512]{0:T(512)S(1)} %dynamic_slice.57, bf16[8,2,2048,4]{2,0,3,1:T(8,128)(2,1)S(1)} %get-tuple-element.405, s32[]{:T(128)S(6)} %select_n.142), kind=kOutput, calls=%fused_computation.42.clone.3 | convolution fusion | flops 603979776 | bytes 2164740 | tf_op jit(solution)/shard_map/while/body/eval_jaxpr/qrvx,yv->qrxy/dot_general | solution.py:109
  1134.7 62.6 %fusion.123 = f32[8,2,4,8192]{3,0,2,1:T(8,128)S(1)} fusion(s32[512]{0:T(512)S(1)} %dynamic_slice.57, bf16[8,2,2048,4]{2,0,3,1:T(8,128)(2,1)S(1)} %get-tuple-element.405, s32[]{:T(128)S(6)} %select_n.142), kind=kOutput, calls=%fused_computation.44.clone.3 | convolution fusion | flops 603979776 | bytes 2164740 | tf_op jit(solution)/shard_map/while/body/eval_jaxpr/qrvx,yv->qrxy/dot_general | solution.py:112
  1197.3 63.4 %fusion.122 = f32[8,2,4,8192]{3,0,2,1:T(8,128)} fusion(s32[512]{0:T(512)S(1)} %dynamic_slice.57, bf16[8,2,2048,4]{2,0,3,1:T(8,128)(2,1)S(1)} %get-tuple-element.405, s32[]{:T(128)S(6)} %select_n.142), kind=kOutput, calls=%fused_computation.42.clone.3 | convolution fusion | flops 603979776 | bytes 2164740 | tf_op jit(solution)/shard_map/while/body/eval_jaxpr/qrvx,yv->qrxy/dot_general | solution.py:109
  1269.1 7.1 scatter_fusion
  1296.5 5.8 all-to-all-start.3
  1304.2 48.2 %all-to-all-done.3 = bf16[32,16,1,16,128]{4,1,3,2,0:T(8,128)(2,1)S(1)} async-done(((bf16[32,16,1,16,128]{4,1,3,2,0:T(8,128)(2,1)}), bf16[32,16,1,16,128]{4,1,3,2,0:T(8,128)(2,1)S(1)}, u32[]{:S(2)}, u32[]{:S(2)}) %all-to-all-start.3) | async-done | bytes 2097184 | tf_op jit(solution)/shard_map/all_to_all | solution.py:137
  1354.9 41.0 %scatter_fusion.1 = f32[16,256,128]{2,0,1:T(8,128)S(1)} fusion(f32[16,256,128]{2,0,1:T(8,128)S(1)} %broadcast_in_dim.13, s32[512]{0:T(512)S(1)} %bitcast.352, f32[512,16,128]{2,1,0:T(8,128)} %bitcast.310), kind=kCustom, calls=%fused_computation.2 | custom fusion | flops 1048576 | bytes 12584960 | tf_op jit(solution)/shard_map/scatter-add | solution.py:164
  (145 shorter events, 102.6 us)
Async XLA Ops:
  7.2 1.8 copy-start.3
  312.9 25.5 %copy-start.4 = (s32[2048]{0:T(1024)S(1)}, s32[2048]{0:T(1024)}, u32[]{:S(2)}) copy-start(s32[2048]{0:T(1024)} %param.12) | copy-start | bytes 24580
  330.8 16.2 %all-to-all-start = ((bf16[16,8,1024]{2,0,1:T(8,128)(2,1)}), bf16[16,8,1024]{2,0,1:T(8,128)(2,1)S(1)}, u32[]{:S(2)}, u32[]{:S(2)}) async-start(bf16[16,8,1024]{2,0,1:T(8,128)(2,1)} %copy.44), calls=%async_computation | async-start | bytes 524288 | tf_op jit(solution)/shard_map/all_to_all | solution.py:59
  338.1 267.7 %reduce-scatter.2.cloned.1.call-start = ((), (), s32[]{:S(2)}) async-start(), calls=%async_computation.5 | async-start | bytes 41943040 | tf_op jit(solution)/shard_map/reduce_scatter | solution.py:79
  371.8 301.0 %all-gather.2.cloned.1.call-start = ((), (), s32[]{:S(2)}) async-start(), calls=%async_computation.6 | async-start | bytes 10485760 | tf_op jit(solution)/shard_map/all_gather | solution.py:83
  610.2 1.6 copy-start.1
  610.2 1.6 copy-start.2
  610.9 1.0 copy-start
  672.8 6.1 copy-start.8
  686.0 10.0 copy-start.5
  690.4 14.9 %all-to-all-start.2 = ((bf16[16,8,1024]{2,0,1:T(8,128)(2,1)}), bf16[16,8,1024]{2,0,1:T(8,128)(2,1)S(1)}, u32[]{:S(2)}, u32[]{:S(2)}) async-start(bf16[16,8,1024]{2,0,1:T(8,128)(2,1)} %copy.54), calls=%async_computation.3 | async-start | bytes 524288 | tf_op jit(solution)/shard_map/all_to_all | solution.py:103
  696.9 8.4 copy-start.6
  705.3 591.2 %all-to-all-start.1 = ((s32[1,32,16]{2,0,1:T(1,128)}), s32[1,32,16]{2,0,1:T(1,128)}, u32[]{:S(2)}, u32[]{:S(2)}) async-start(s32[1,32,16]{2,0,1:T(1,128)} %bitcast.20), calls=%async_computation.2 | async-start | bytes 32768 | tf_op jit(solution)/shard_map/all_to_all | solution.py:151
  1268.1 1.0 copy-start.7
  1296.5 55.9 %all-to-all-start.3 = ((bf16[32,16,1,16,128]{4,1,3,2,0:T(8,128)(2,1)}), bf16[32,16,1,16,128]{4,1,3,2,0:T(8,128)(2,1)S(1)}, u32[]{:S(2)}, u32[]{:S(2)}) async-start(bf16[32,16,1,16,128]{4,1,3,2,0:T(8,128)(2,1)} %constant_dynamic-update-slice_fusion), calls=%async_computation.4 | async-start | bytes 4194304 | tf_op jit(solution)/shard_map/all_to_all | solution.py:137
Sparse Core Ops, SparseCore 0:
  371.9 233.7 reduce-scatter.1
  614.4 58.2 all-gather.1
